TPU v7x, 512 devices: a whole 4x8x8 slice. The times are simulated.
512 devices in a mesh: tm: 64 (over z, y), chan: 8 (over x, core).
Axes of the slice: x: 4, y: 8, z: 8, core: 2. Of those that a mesh axis runs over, the one named last changes fastest.
Arguments:
- values: bfloat16 [16384, 4096], P('tm', 'chan'), may hold values from -6 to 6
- gates: bfloat16 [16384, 4096], P('tm', 'chan'), may hold values from -6 to 6
- cotangent: bfloat16 [16384, 4096], P('tm', 'chan'), may hold values from -6 to 6
- kernel_taps: bfloat16 [256, 4096], P(None, 'chan'), may hold values from -0.375 to 0.375
- value_weight: bfloat16 [4096, 4096], P('tm', 'chan'), may hold values from -0.09375 to 0.09375
- gate_weight: bfloat16 [4096, 4096], P('tm', 'chan'), may hold values from -0.09375 to 0.09375
Outputs:
- grad_input: bfloat16 [16384, 4096], P('tm', 'chan')
- kernel_grad: float32 [256, 4096], P('tm', 'chan')
All inputs are finite; a program needn't handle non-finite values.
Results may differ from a plain program's by a relative error of at most 0.017.
Values may be sent and summed in bfloat16 or wider, within the bound.
A program may use at most 64 MiB of HBM per device.

v0:
```python
import math
import jax
import jax.numpy as jnp
import numpy as np
from jax import lax
from jax.sharding import PartitionSpec as P


def from_behind(value, axis, steps):
    count = lax.axis_size(axis)
    initial, last = (max(0, -steps), min(count, count - steps))
    return lax.ppermute(value, axis, [(source, source + steps) for source in range(initial, last)])


def contract_rows(left, weight_rows):
    return lax.dot_general(
        left, weight_rows, (((1,), (1,)), ((), ())), preferred_element_type=jnp.float32
    )


def forward_tables(length):
    freq_count = length // 2 + 1
    phase = np.arange(freq_count)[:, None] * np.arange(length)[None, :] % length
    angle = phase * (2.0 * np.pi / length)
    return (
        jnp.asarray(np.cos(angle), dtype=jnp.float32),
        jnp.asarray(np.sin(angle), dtype=jnp.float32),
    )


def inverse_tables(first, count, length):
    freq_count = length // 2 + 1
    freqs = np.arange(freq_count)
    phase = (first + np.arange(count))[:, None] * freqs[None, :] % length
    angle = phase * (2.0 * np.pi / length)
    weight = np.where((freqs == 0) | (freqs == length // 2), 1.0, 2.0) / length
    return (
        jnp.asarray(np.cos(angle) * weight[None, :], dtype=jnp.float32),
        jnp.asarray(np.sin(angle) * weight[None, :], dtype=jnp.float32),
    )


def precise_dot(left, right):
    return jnp.dot(left, right, precision=lax.Precision.HIGHEST, preferred_element_type=jnp.float32)


def back_to_time(first, count, length, real_part, imag_part):
    cos_inv, sin_inv = inverse_tables(first, count, length)
    return precise_dot(cos_inv, real_part) - precise_dot(sin_inv, imag_part)


def body(values, gates, cotangent, kernel_taps, value_weight, gate_weight):
    row_count, chan_count = values.shape
    span_len = kernel_taps.shape[0]
    window_len = row_count + span_len
    grad_conv = (cotangent.astype(jnp.float32) * gates.astype(jnp.float32)).astype(jnp.bfloat16)
    value_rim = from_behind(values[row_count - span_len + 1 :], "tm", 1)
    grad_rim = from_behind(grad_conv[: span_len - 1], "tm", -1)
    zero_row = jnp.zeros((1, chan_count), jnp.bfloat16)
    value_window = jnp.concatenate([zero_row, value_rim, values], 0)
    grad_window = jnp.concatenate([grad_conv, grad_rim, zero_row], 0)
    grad_padded = jnp.concatenate([jnp.zeros((span_len, chan_count), jnp.bfloat16), grad_conv], 0)
    taps_padded = jnp.concatenate(
        [kernel_taps, jnp.zeros((row_count, chan_count), jnp.bfloat16)], 0
    )
    joined_time = jnp.concatenate([value_window, grad_window, grad_padded, taps_padded], 1).astype(
        jnp.float32
    )
    cos_fwd, sin_fwd = forward_tables(window_len)
    real_all = precise_dot(cos_fwd, joined_time)
    imag_all = -precise_dot(sin_fwd, joined_time)
    value_re = real_all[:, :chan_count]
    value_im = imag_all[:, :chan_count]
    grad_re = real_all[:, chan_count : 2 * chan_count]
    grad_im = imag_all[:, chan_count : 2 * chan_count]
    pad_re = real_all[:, 2 * chan_count : 3 * chan_count]
    pad_im = imag_all[:, 2 * chan_count : 3 * chan_count]
    taps_re = real_all[:, 3 * chan_count :]
    taps_im = imag_all[:, 3 * chan_count :]
    conv_out = back_to_time(
        span_len,
        row_count,
        window_len,
        value_re * taps_re - value_im * taps_im,
        value_re * taps_im + value_im * taps_re,
    )
    grad_value = back_to_time(
        0,
        row_count,
        window_len,
        grad_re * taps_re + grad_im * taps_im,
        grad_im * taps_re - grad_re * taps_im,
    ).astype(jnp.bfloat16)
    norm_scale = 1.0 / math.sqrt(row_count * lax.axis_size("tm"))
    kernel_part = (
        back_to_time(
            0,
            span_len,
            window_len,
            pad_re * value_re + pad_im * value_im,
            pad_im * value_re - pad_re * value_im,
        )
        * norm_scale
    )
    grad_gate = (cotangent.astype(jnp.float32) * conv_out).astype(jnp.bfloat16)
    kernel_grad = lax.psum_scatter(kernel_part, "tm", scatter_dimension=0, tiled=True)
    terms = contract_rows(grad_value, lax.all_gather(value_weight, "tm", axis=0, tiled=True))
    terms = terms + contract_rows(grad_gate, lax.all_gather(gate_weight, "tm", axis=0, tiled=True))
    grad_input = lax.psum_scatter(
        terms.astype(jnp.bfloat16), "chan", scatter_dimension=1, tiled=True
    )
    return (grad_input, kernel_grad)


def solution(mesh):
    placed = (
        P("tm", "chan"),
        P("tm", "chan"),
        P("tm", "chan"),
        P(None, "chan"),
        P("tm", "chan"),
        P("tm", "chan"),
    )
    return jax.shard_map(
        body,
        mesh=mesh,
        in_specs=placed,
        out_specs=(P("tm", "chan"), P("tm", "chan")),
        check_vma=False,
    )
```

profile of v0, /device:TPU:8, one launch (start us, length us, event | category | flops | bytes accessed | tf_op | source)
XLA Modules:
  0.0 391.1 jit_solution(17819899406508750567)
XLA Ops:
  8.7 1.0 slice.30
  9.7 3.6 collective-permute-start
  13.3 1.1 fusion.34
  14.4 5.6 %collective-permute-start.1 = (bf16[255,512]{1,0:T(8,128)(2,1)S(1)}, bf16[255,512]{1,0:T(8,128)(2,1)S(1)}, u32[]{:S(2)}, u32[]{:S(2)}) collective-permute-start(bf16[255,512]{1,0:T(8,128)(2,1)S(1)} %bitcast.28), channel_id=1, source_target_pairs={{8,0},{16,8},{24,16},{32,24},{40,32},{48,40},{56,48},{64,56},{72,6... | collective-permute-start | bytes 783368 | tf_op jit(solution)/shard_map/ppermute | solution.py:12
  20.0 1.3 collective-permute-done
  21.3 2.8 collective-permute-done.1
  24.1 4.9 %fusion.6 = bf16[512,2048]{1,0:T(8,128)(2,1)S(1)} fusion(bf16[256,512]{1,0:T(8,128)(2,1)} %param.17, bf16[256,512]{1,0:T(8,128)(2,1)S(1)} %fusion.34, bf16[1,512]{1,0:T(2,128)(2,1)S(1)} %broadcast_in_dim.3, bf16[255,512]{1,0:T(8,128)(2,1)S(1)} %collective-permute-done.1, bf16[256,512]{1,0:T(8,128)(2,1)} %param.14, bf16[255,512]{1,0:T(8,128)(2,1)S(1)} %collective-permute-done), kind=kLoop, calls=%fused_computation.11 | loop fusion | flops 23068672 | bytes 3406848 | tf_op jit(solution)/shard_map/concatenate | solution.py:66
  29.0 1.9 fusion.4
  30.9 1.9 fusion.59
  32.8 1.5 fusion.16
  34.3 1.5 fusion.30
  35.8 1.1 fusion.23
  37.0 1.5 fusion.12
  38.5 2.3 fusion.8
  41.1 2.4 fusion.11
  43.5 59.0 %all-gather.3.cloned.1.call-done = bf16[4096,512]{1,0:T(8,128)(2,1)} async-done(((bf16[64,512]{1,0:T(8,128)(2,1)}), bf16[4096,512]{1,0:T(8,128)(2,1)}) %all-gather.3.cloned.1.call-update) | async-done | bytes 4194320 | tf_op jit(solution)/shard_map/all_gather | solution.py:107
  102.5 5.5 %fusion.60 = f32[256,4096]{1,0:T(8,128)} fusion(bf16[512,256]{1,0:T(8,128)(2,1)S(1)} %fusion.12, bf16[4096,512]{1,0:T(8,128)(2,1)} %all-gather.3.cloned.1.call-done), kind=kOutput, calls=%fused_computation.70 | convolution fusion | flops 1073741824 | bytes 8650752 | tf_op jit(solution)/shard_map/dot_general | solution.py:16
  108.0 81.5 %all-gather.5.cloned.1.call-done = bf16[4096,512]{1,0:T(8,128)(2,1)} async-done(((bf16[64,512]{1,0:T(8,128)(2,1)}), bf16[4096,512]{1,0:T(8,128)(2,1)}) %all-gather.5.cloned.1.call-update) | async-done | bytes 4194320 | tf_op jit(solution)/shard_map/all_gather | solution.py:108
  189.5 6.1 %fusion = bf16[256,4096]{1,0:T(8,128)(2,1)} fusion(f32[256,4096]{1,0:T(8,128)} %fusion.60, bf16[256,512]{1,0:T(8,128)(2,1)S(1)} %fusion.11, bf16[4096,512]{1,0:T(8,128)(2,1)} %all-gather.5.cloned.1.call-done), kind=kOutput, calls=%fused_computation.3 | convolution fusion | flops 1075838976 | bytes 10747904 | tf_op jit(solution)/shard_map/dot_general | solution.py:16
  195.6 1.3 dynamic-slice
  197.5 147.6 %all-reduce.5.cloned.1.call-done = f32[256,512]{0,1:T(8,128)} async-done(((f32[256,512]{0,1:T(8,128)}), f32[256,512]{0,1:T(8,128)}) %all-reduce.5.cloned.1.call-update) | async-done | bytes 524304
  345.1 1.1 constant_dynamic-slice_fusion
  346.2 0.7 copy.17
  346.9 37.6 %reduce-scatter.3.cloned.1.call-done = bf16[256,512]{1,0:T(8,128)(2,1)} async-done(((bf16[256,4096]{1,0:T(8,128)(2,1)}), bf16[256,512]{1,0:T(8,128)(2,1)}) %reduce-scatter.3.cloned.1.call-update) | async-done | bytes 262160 | tf_op jit(solution)/shard_map/reduce_scatter | solution.py:109
  (23 shorter events, 1.8 us)
Async XLA Ops:
  7.2 95.4 %all-gather.3.cloned.1.call-start = ((), (), s32[]{:S(2)}) async-start(), calls=%async_computation.1 | async-start | bytes 4259840 | tf_op jit(solution)/shard_map/all_gather | solution.py:107
  7.9 181.6 %all-gather.5.cloned.1.call-start = ((), (), s32[]{:S(2)}) async-start(), calls=%async_computation.2 | async-start | bytes 4259840 | tf_op jit(solution)/shard_map/all_gather | solution.py:108
  8.6 336.5 %all-reduce.5.cloned.1.call-start = ((), (), s32[]{:S(2)}) async-start(), calls=%async_computation.4 | async-start | bytes 1048576
  9.7 19.3 %copy-start.5 = (f32[257,512]{1,0:T(8,128)S(1)}, f32[257,512]{1,0:T(8,128)}, u32[]{:S(2)}) copy-start(f32[257,512]{1,0:T(8,128)} %constant.18.clone) | copy-start | bytes 1579012
  9.7 11.6 %collective-permute-start = (bf16[255,512]{1,0:T(8,128)(2,1)S(1)}, bf16[255,512]{1,0:T(8,128)(2,1)S(1)}, u32[]{:S(2)}, u32[]{:S(2)}) collective-permute-start(bf16[255,512]{1,0:T(8,128)(2,1)S(1)} %slice.30), channel_id=1, source_target_pairs={{0,8},{8,16},{16,24},{24,32},{32,40},{40,48},{48,56},{56,64},{64,7... | collective-permute-start | bytes 783368 | tf_op jit(solution)/shard_map/ppermute | solution.py:12
  14.4 9.7 %collective-permute-start.1 = (bf16[255,512]{1,0:T(8,128)(2,1)S(1)}, bf16[255,512]{1,0:T(8,128)(2,1)S(1)}, u32[]{:S(2)}, u32[]{:S(2)}) collective-permute-start(bf16[255,512]{1,0:T(8,128)(2,1)S(1)} %bitcast.28), channel_id=1, source_target_pairs={{8,0},{16,8},{24,16},{32,24},{40,32},{48,40},{56,48},{64,56},{72,6... | collective-permute-start | bytes 783368 | tf_op jit(solution)/shard_map/ppermute | solution.py:12
  29.0 1.9 copy-start.3
  30.9 7.6 %copy-start = (f32[257,2048]{1,0:T(8,128)}, f32[257,2048]{1,0:T(8,128)S(1)}, u32[]{:S(2)}) copy-start(f32[257,2048]{1,0:T(8,128)S(1)} %fusion.4) | copy-start | bytes 6316036
  30.9 1.9 copy-start.2
  32.8 3.0 copy-start.6
  34.3 2.6 copy-start.1
  37.0 4.1 %copy-start.4 = (bf16[256,512]{1,0:T(8,128)(2,1)S(1)}, bf16[256,512]{1,0:T(8,128)(2,1)}, u32[]{:S(2)}) copy-start(bf16[256,512]{1,0:T(8,128)(2,1)} %param.16) | copy-start | bytes 786436
  40.8 343.7 %reduce-scatter.3.cloned.1.call-start = ((), (), s32[]{:S(2)}) async-start(), calls=%async_computation.3 | async-start | bytes 2359296 | tf_op jit(solution)/shard_map/reduce_scatter | solution.py:109
Sparse Core Ops, SparseCore 0:
  11.1 91.4 all-gather.2
  105.6 83.8 all-gather.4
  192.7 152.4 all-reduce.4
  348.6 35.8 reduce-scatter.2
where the time goes:
time: 391 us
  waiting for transfers between devices  331 us (85%)
  matrix products  25.6 us (7%)
  between operations  14.6 us (4%)
  starting transfers between devices  9.54 us (2%)
  other arithmetic  5.97 us (2%)
  local copies, waits for them, and re-layouts  4.12 us (1%)
    unnamed x5, waiting for transfers between devices  149 us
    all_gather x1, waiting for transfers between devices, body(): lax.all_gather(gate_weight, 'tm', axis=0, tiled=True)  81.5 us
    all_gather x1, waiting for transfers between devices, body(): lax.all_gather(value_weight, 'tm', axis=0, tiled=True)  59 us
    reduce_scatter x1, waiting for transfers between devices, body(): lax.psum_scatter(terms.astype(jnp.bfloat16), 'chan', scatter_dimension=1,...  37.6 us
    dot_general x8, matrix products, precise_dot(): jnp.dot(left, right, precision=lax.Precision.HIGHEST, preferred_element_t...  14.1 us
    dot_general x2, matrix products, contract_rows(): lax.dot_general(left, weight_rows, (((1,), (1,)), ((), ())), preferred_el...  11.6 us
    ppermute x2, starting transfers between devices, from_behind(): lax.ppermute(value, axis, [(source, source + steps) for source in range(i...  9.17 us
  transfers between devices with their start and end apart: 6, of which 6 were waited for; matrix products, arithmetic and copies ran while one was open for 9% of the time, Pallas kernels for 0%

commit v1 on v0

--- a/solution.py
+++ b/solution.py
@@ -4,6 +4,11 @@
 import numpy as np
 from jax import lax
 from jax.sharding import PartitionSpec as P
+
+
+def swapped_in(array, axis, along):
+    sent = jnp.stack([array] * lax.axis_size(axis))
+    return jnp.concatenate(lax.all_to_all(sent, axis, 0, 0), axis=along)
 
 
 def from_behind(value, axis, steps):
@@ -104,7 +109,7 @@
     )
     grad_gate = (cotangent.astype(jnp.float32) * conv_out).astype(jnp.bfloat16)
     kernel_grad = lax.psum_scatter(kernel_part, "tm", scatter_dimension=0, tiled=True)
-    terms = contract_rows(grad_value, lax.all_gather(value_weight, "tm", axis=0, tiled=True))
+    terms = contract_rows(grad_value, swapped_in(value_weight, "tm", 0))
     terms = terms + contract_rows(grad_gate, lax.all_gather(gate_weight, "tm", axis=0, tiled=True))
     grad_input = lax.psum_scatter(
         terms.astype(jnp.bfloat16), "chan", scatter_dimension=1, tiled=True

time: 391 us -> 400 us (1.023)
  starting transfers between devices: 9.54 us -> 23.2 us
  waiting for transfers between devices: 331 us -> 321 us
    ppermute x2, waiting for transfers between devices: 4.1 us -> 121 us  [from_behind(): lax.ppermute(value, axis, [(source, source + steps) for source in range(i...]
    all_gather x1, waiting for transfers between devices: 81.5 us -> 13.6 us  [body(): lax.all_gather(gate_weight, 'tm', axis=0, tiled=True)]
    all_gather x1 -> x0, waiting for transfers between devices: 59 us -> none  [body(): lax.all_gather(value_weight, 'tm', axis=0, tiled=True)]
    all_to_all x0 -> x1, starting transfers between devices: none -> 16.9 us  [swapped_in(): return jnp.concatenate(lax.all_to_all(sent, axis, 0, 0), axis=along)]
    unnamed x5 -> x4, waiting for transfers between devices: 149 us -> 148 us
  transfers between devices with their start and end apart: 6 -> 6, of which waited for: 6 -> 4; matrix products, arithmetic and copies ran while one was open for 9% -> 10% of each run, Pallas kernels for 0% -> 0%
where the time goes in v1:
time: 400 us; the launch traced here: 399 us
  waiting for transfers between devices  321 us (80%)
  matrix products  27.1 us (7%)
  starting transfers between devices  23.2 us (6%)
  between operations  14.7 us (4%)
  other arithmetic  7.11 us (2%)
  local copies, waits for them, and re-layouts  6.49 us (2%)
    unnamed x4, waiting for transfers between devices  148 us
    ppermute x2, waiting for transfers between devices, from_behind(): lax.ppermute(value, axis, [(source, source + steps) for source in range(i...  121 us
    reduce_scatter x1, waiting for transfers between devices, body(): lax.psum_scatter(terms.astype(jnp.bfloat16), 'chan', scatter_dimension=1,...  37.8 us
    all_to_all x1, starting transfers between devices, swapped_in(): return jnp.concatenate(lax.all_to_all(sent, axis, 0, 0), axis=along)  16.9 us
    dot_general x8, matrix products, precise_dot(): jnp.dot(left, right, precision=lax.Precision.HIGHEST, preferred_element_t...  15.5 us
    all_gather x1, waiting for transfers between devices, body(): lax.all_gather(gate_weight, 'tm', axis=0, tiled=True)  13.6 us
    dot_general x2, matrix products, contract_rows(): lax.dot_general(left, weight_rows, (((1,), (1,)), ((), ())), preferred_el...  11.6 us
  transfers between devices with their start and end apart: 6, of which 4 were waited for; matrix products, arithmetic and copies ran while one was open for 10% of the time, Pallas kernels for 0%

profile of v1, /device:TPU:8, one launch (start us, length us, event | category | flops | bytes accessed | tf_op | source)
XLA Modules:
  0.0 399.4 jit_solution(12722056661733368587)
XLA Ops:
  7.2 0.7 all-gather.2.cloned.1.call-update
  7.9 3.3 stack.2
  11.2 16.9 %all-to-all-start = ((bf16[64,64,512]{2,1,0:T(8,128)(2,1)}), bf16[64,64,512]{2,1,0:T(8,128)(2,1)}, u32[]{:S(2)}, u32[]{:S(2)}) async-start(bf16[64,64,512]{2,1,0:T(8,128)(2,1)} %stack.2), calls=%async_computation | async-start | bytes 8388608 | tf_op jit(solution)/shard_map/all_to_all | solution.py:11
  28.3 3.5 collective-permute-start
  31.9 2.5 collective-permute-start.1
  34.4 121.1 %collective-permute-done = bf16[255,512]{1,0:T(8,128)(2,1)S(1)} collective-permute-done((bf16[255,512]{1,0:T(8,128)(2,1)S(1)}, bf16[255,512]{1,0:T(8,128)(2,1)S(1)}, u32[]{:S(2)}, u32[]{:S(2)}) %collective-permute-start) | collective-permute-done | bytes 261152 | tf_op jit(solution)/shard_map/ppermute | solution.py:17
  155.5 7.0 %fusion.6 = bf16[512,2048]{1,0:T(8,128)(2,1)S(1)} fusion(bf16[256,512]{1,0:T(8,128)(2,1)S(1)} %copy-done.10, bf16[256,512]{1,0:T(8,128)(2,1)S(1)} %fusion.34, bf16[1,512]{1,0:T(2,128)(2,1)S(1)} %broadcast_in_dim.3, bf16[255,512]{1,0:T(8,128)(2,1)S(1)} %collective-permute-done.1, bf16[256,512]{1,0:T(8,128)(2,1)S(1)} %copy-done.6, ...), kind=kLoop, calls=%fused_computation.11 | loop fusion | flops 23068672 | bytes 3406848 | tf_op jit(solution)/shard_map/concatenate | solution.py:71
  162.6 1.9 fusion.4
  164.5 1.9 fusion.59
  166.4 1.5 fusion.16
  167.9 2.3 fusion.8
  170.3 0.2 reduce-scatter.3.cloned.1.call-start
  170.5 2.9 fusion.30
  173.4 2.5 fusion.23
  175.9 1.5 fusion.12
  177.4 1.1 fusion.11
  178.5 5.5 %fusion.60 = f32[256,4096]{1,0:T(8,128)} fusion(bf16[512,256]{1,0:T(8,128)(2,1)S(1)} %fusion.12, bf16[4096,512]{1,0:T(8,128)(2,1)} %bitcast.1), kind=kOutput, calls=%fused_computation.70 | convolution fusion | flops 1073741824 | bytes 8650752 | tf_op jit(solution)/shard_map/dot_general | solution.py:21
  184.0 13.6 %all-gather.2.cloned.1.call-done = bf16[4096,512]{1,0:T(8,128)(2,1)} async-done(((bf16[64,512]{1,0:T(8,128)(2,1)}), bf16[4096,512]{1,0:T(8,128)(2,1)}) %all-gather.2.cloned.1.call-update) | async-done | bytes 4194320 | tf_op jit(solution)/shard_map/all_gather | solution.py:113
  197.6 6.1 %fusion = bf16[256,4096]{1,0:T(8,128)(2,1)} fusion(f32[256,4096]{1,0:T(8,128)} %fusion.60, bf16[256,512]{1,0:T(8,128)(2,1)S(1)} %fusion.11, bf16[4096,512]{1,0:T(8,128)(2,1)} %all-gather.2.cloned.1.call-done), kind=kOutput, calls=%fused_computation.3 | convolution fusion | flops 1075838976 | bytes 10747904 | tf_op jit(solution)/shard_map/dot_general | solution.py:21
  203.7 1.3 dynamic-slice
  205.7 147.6 %all-reduce.5.cloned.1.call-done = f32[256,512]{0,1:T(8,128)} async-done(((f32[256,512]{0,1:T(8,128)}), f32[256,512]{0,1:T(8,128)}) %all-reduce.5.cloned.1.call-update) | async-done | bytes 524304
  353.3 1.1 constant_dynamic-slice_fusion
  354.4 0.7 copy.17
  355.1 37.8 %reduce-scatter.3.cloned.1.call-done = bf16[256,512]{1,0:T(8,128)(2,1)} async-done(((bf16[256,4096]{1,0:T(8,128)(2,1)}), bf16[256,512]{1,0:T(8,128)(2,1)}) %reduce-scatter.3.cloned.1.call-update) | async-done | bytes 262160 | tf_op jit(solution)/shard_map/reduce_scatter | solution.py:114
  (31 shorter events, 0.3 us)
Async XLA Ops:
  7.2 190.4 %all-gather.2.cloned.1.call-start = ((), (), s32[]{:S(2)}) async-start(), calls=%async_computation.2 | async-start | bytes 4259840 | tf_op jit(solution)/shard_map/all_gather | solution.py:113
  11.2 17.0 %copy-start.6 = (bf16[256,512]{1,0:T(8,128)(2,1)S(1)}, bf16[256,512]{1,0:T(8,128)(2,1)}, u32[]{:S(2)}) copy-start(bf16[256,512]{1,0:T(8,128)(2,1)} %param.14) | copy-start | bytes 786436
  11.2 20.6 %copy-start.5 = (bf16[256,512]{1,0:T(8,128)(2,1)S(1)}, bf16[256,512]{1,0:T(8,128)(2,1)}, u32[]{:S(2)}) copy-start(bf16[256,512]{1,0:T(8,128)(2,1)} %param.16) | copy-start | bytes 786436
  11.2 20.6 %copy-start.9 = (bf16[256,512]{1,0:T(8,128)(2,1)S(1)}, bf16[256,512]{1,0:T(8,128)(2,1)}, u32[]{:S(2)}) copy-start(bf16[256,512]{1,0:T(8,128)(2,1)} %param.15) | copy-start | bytes 786436
  11.2 144.3 %copy-start.10 = (bf16[256,512]{1,0:T(8,128)(2,1)S(1)}, bf16[256,512]{1,0:T(8,128)(2,1)}, u32[]{:S(2)}) copy-start(bf16[256,512]{1,0:T(8,128)(2,1)} %param.17) | copy-start | bytes 786436
  11.2 167.3 %all-to-all-start = ((bf16[64,64,512]{2,1,0:T(8,128)(2,1)}), bf16[64,64,512]{2,1,0:T(8,128)(2,1)}, u32[]{:S(2)}, u32[]{:S(2)}) async-start(bf16[64,64,512]{2,1,0:T(8,128)(2,1)} %stack.2), calls=%async_computation | async-start | bytes 8388608 | tf_op jit(solution)/shard_map/all_to_all | solution.py:11
  28.1 325.2 %all-reduce.5.cloned.1.call-start = ((), (), s32[]{:S(2)}) async-start(), calls=%async_computation.4 | async-start | bytes 1048576
  28.3 134.3 %copy-start.7 = (f32[257,512]{1,0:T(8,128)S(1)}, f32[257,512]{1,0:T(8,128)}, u32[]{:S(2)}) copy-start(f32[257,512]{1,0:T(8,128)} %constant.18.clone) | copy-start | bytes 1579012
  28.3 127.2 %collective-permute-start = (bf16[255,512]{1,0:T(8,128)(2,1)S(1)}, bf16[255,512]{1,0:T(8,128)(2,1)S(1)}, u32[]{:S(2)}, u32[]{:S(2)}) collective-permute-start(bf16[255,512]{1,0:T(8,128)(2,1)S(1)} %slice.30), channel_id=1, source_target_pairs={{0,8},{8,16},{16,24},{24,32},{32,40},{40,48},{48,56},{56,64},{64,7... | collective-permute-start | bytes 783368 | tf_op jit(solution)/shard_map/ppermute | solution.py:17
  31.9 123.6 %collective-permute-start.1 = (bf16[255,512]{1,0:T(8,128)(2,1)S(1)}, bf16[255,512]{1,0:T(8,128)(2,1)S(1)}, u32[]{:S(2)}, u32[]{:S(2)}) collective-permute-start(bf16[255,512]{1,0:T(8,128)(2,1)S(1)} %bitcast.29), channel_id=1, source_target_pairs={{8,0},{16,8},{24,16},{32,24},{40,32},{48,40},{56,48},{64,56},{72,6... | collective-permute-start | bytes 783368 | tf_op jit(solution)/shard_map/ppermute | solution.py:17
  162.6 1.9 copy-start.4
  164.5 3.4 copy-start
  164.5 1.9 copy-start.3
  166.4 1.5 copy-start.2
  170.3 222.6 %reduce-scatter.3.cloned.1.call-start = ((), (), s32[]{:S(2)}) async-start(), calls=%async_computation.3 | async-start | bytes 2359296 | tf_op jit(solution)/shard_map/reduce_scatter | solution.py:114
  170.5 5.4 %copy-start.1 = (f32[257,2048]{1,0:T(8,128)S(1)}, f32[257,2048]{1,0:T(8,128)}, u32[]{:S(2)}) copy-start(f32[257,2048]{1,0:T(8,128)} %copy-done) | copy-start | bytes 6316036
  173.4 4.0 copy-start.8
Sparse Core Ops, SparseCore 0:
  11.1 186.4 all-gather.1
  200.8 152.4 all-reduce.4
  357.0 35.8 reduce-scatter.2
